TPU v7x, 128 devices: a whole 4x4x4 slice. The times are simulated.
128 devices in a mesh: row: 16 (over x, z), col: 8 (over y, core).
Axes of the slice: x: 4, y: 4, z: 4, core: 2. Of those that a mesh axis runs over, the one named last changes fastest.
Arguments:
- diag_one: float32 [512, 512], P('row')
- coupling: float32 [512, 512], P('row'), may hold values from -0.25 to 0.25
- diag_two: float32 [512, 512], P('row')
- off_one: float32 [32768, 512], P(('row', 'col')), may hold values from -2 to 2
- off_two: float32 [32768, 512], P(('row', 'col')), may hold values from -2 to 2
- targets: float32 [16384, 128, 128], P(('row', 'col')), may hold values from -6 to 6
- pattern: int32 [16384, 2], P(('row', 'col')), may hold values from 0 to 255, as said below
Outputs:
- lower_one: float32 [32768, 512], P(('row', 'col'))
- lower_two: float32 [32768, 512], P(('row', 'col'))
- updated: float32 [16384, 128, 128], P(('row', 'col'))
Inputs may be any that keep to these rules, and one draw needn't show every extreme that they name: Rows of pattern come in groups of 128; group f belongs to grid position (r, c) = (f // 8, f % 8) of the row and col axes (sizes 16, 8). Its block rows i lie in r * 8 * 2 to (r + 1) * 8 * 2 - 1; its block columns j satisfy (j // 2) % 8 == c; always j <= i. Pairs may repeat.
All inputs are finite; a program needn't handle non-finite values.
Results may differ from a plain program's by a relative error of at most 0.00005.
Values sent between devices are 32-bit elements; how exact they have to be, the bound alone decides.
No kernel may reach another device: no remote copies, remote signals or barrier semaphores. Data moves between devices by JAX's collectives and lax.ppermute only.
A program may use at most 128 MiB of HBM per device.

v0:
```python
import jax
import jax.numpy as jnp
from jax import lax
from jax.sharding import PartitionSpec as P


def make_solver(chol):

    def apply_solve(rows):
        return lax.linalg.triangular_solve(
            chol, rows, left_side=False, lower=True, transpose_a=True
        )

    return apply_solve


def pair_updates(targets, pattern, row_one, row_two, col_one, col_two, shard_blocks):
    highest = lax.Precision.HIGHEST
    block = targets.shape[1]
    width = row_one.shape[1]
    ncol = lax.axis_size("col")
    span = row_one.shape[0] // block
    row_blocks_one = row_one.reshape(span, block, width)
    row_blocks_two = row_two.reshape(span, block, width)
    col_span = col_one.shape[0] // block
    col_blocks_one = col_one.reshape(col_span, block, width)
    col_blocks_two = col_two.reshape(col_span, block, width)
    local_row = pattern[:, 0] % span
    global_col = pattern[:, 1]
    local_col = global_col // (shard_blocks * ncol) * shard_blocks + global_col % shard_blocks
    groups = targets.shape[0] // 16
    tiles = targets.reshape(groups, 16, block, block)

    def one_group(items):
        tile, row_id, col_id = items
        first = jnp.einsum(
            "kaw,kbw->kab", row_blocks_one[row_id], col_blocks_one[col_id], precision=highest
        )
        second = jnp.einsum(
            "kaw,kbw->kab", row_blocks_two[row_id], col_blocks_two[col_id], precision=highest
        )
        return tile - (first + second)

    result = lax.map(
        one_group, (tiles, local_row.reshape(groups, 16), local_col.reshape(groups, 16))
    )
    return result.reshape(targets.shape)


def shards(diag_one, coupling, diag_two, off_one, off_two, targets, pattern):
    highest = lax.Precision.HIGHEST
    block = targets.shape[1]
    shard_blocks = off_one.shape[0] // block
    full_one, full_coupling, full_two = (
        lax.all_gather(diag_one, "row", axis=0, tiled=True),
        lax.all_gather(coupling, "row", axis=0, tiled=True),
        lax.all_gather(diag_two, "row", axis=0, tiled=True),
    )
    chol_one = jnp.linalg.cholesky(full_one)
    solve_one = make_solver(chol_one)
    lower_coupling = solve_one(full_coupling)
    lower_one = solve_one(off_one)
    schur = full_two - jnp.dot(lower_coupling, lower_coupling.T, precision=highest)
    chol_two = jnp.linalg.cholesky(schur)
    shifted = off_two - jnp.dot(lower_one, lower_coupling.T, precision=highest)
    lower_two = make_solver(chol_two)(shifted)
    row_one, row_two = (
        lax.all_gather(lower_one, "col", axis=0, tiled=True),
        lax.all_gather(lower_two, "col", axis=0, tiled=True),
    )
    col_one, col_two = (
        lax.all_gather(lower_one, "row", axis=0, tiled=True),
        lax.all_gather(lower_two, "row", axis=0, tiled=True),
    )
    updated = pair_updates(targets, pattern, row_one, row_two, col_one, col_two, shard_blocks)
    return (lower_one, lower_two, updated)


def solution(mesh):
    return jax.shard_map(
        shards,
        mesh=mesh,
        in_specs=(
            P("row", None),
            P("row", None),
            P("row", None),
            P(("row", "col"), None),
            P(("row", "col"), None),
            P(("row", "col"), None, None),
            P(("row", "col"), None),
        ),
        out_specs=(P(("row", "col"), None), P(("row", "col"), None), P(("row", "col"), None, None)),
        check_vma=False,
    )
```

profile of v0, /device:TPU:0, one launch (start us, length us, event | category | flops | bytes accessed | tf_op | source)
XLA Modules:
  0.0 922.9 jit_solution(18037836685526295646)
XLA Ops:
  9.4 45.8 %all-gather.8.cloned.1.call-done = f32[512,512]{1,0:T(8,128)} async-done(((f32[32,512]{1,0:T(8,128)}), f32[512,512]{1,0:T(8,128)}) %all-gather.8.cloned.1.call-update) | async-done | bytes 1048592 | tf_op jit(solution)/shard_map/all_gather | solution.py:55
  58.3 11.7 %cholesky.286 = f32[128,128]{1,0:T(8,128)S(1)} custom-call(f32[128,128]{1,0:T(8,128)S(1)} %cholesky.426), custom_call_target="Cholesky" | custom-call | tf_op jit(solution)/shard_map/jit(cholesky)/cholesky | solution.py:59
  70.0 9.8 %custom-call.31 = f32[1,128,128]{1,2,0:T(8,128)S(1)} custom-call(f32[1,128,128]{2,1,0:T(8,128)S(1)} %get-tuple-element.162), custom_call_target="InvertDiagBlocksLowerTriangular" | custom-call | tf_op jit(solution)/shard_map/jit(cholesky)/cholesky | solution.py:59
  80.7 11.7 %cholesky.305 = f32[128,128]{1,0:T(8,128)S(1)} custom-call(f32[128,128]{1,0:T(8,128)S(1)} %cholesky.430), custom_call_target="Cholesky" | custom-call | tf_op jit(solution)/shard_map/jit(cholesky)/cholesky | solution.py:59
  92.4 10.0 %custom-call.32 = f32[1,128,128]{1,2,0:T(8,128)S(1)} custom-call(f32[1,128,128]{2,1,0:T(8,128)S(1)} %get-tuple-element.159), custom_call_target="InvertDiagBlocksLowerTriangular" | custom-call | tf_op jit(solution)/shard_map/jit(cholesky)/cholesky | solution.py:59
  103.1 11.7 %cholesky.326 = f32[128,128]{1,0:T(8,128)S(1)} custom-call(f32[128,128]{1,0:T(8,128)S(1)} %cholesky.435), custom_call_target="Cholesky" | custom-call | tf_op jit(solution)/shard_map/jit(cholesky)/cholesky | solution.py:59
  115.5 9.8 %custom-call.33 = f32[1,128,128]{1,2,0:T(8,128)S(1)} custom-call(f32[1,128,128]{2,1,0:T(8,128)S(1)} %get-tuple-element.156), custom_call_target="InvertDiagBlocksLowerTriangular" | custom-call | tf_op jit(solution)/shard_map/jit(cholesky)/cholesky | solution.py:59
  125.9 11.7 %cholesky.343 = f32[128,128]{1,0:T(8,128)S(1)} custom-call(f32[128,128]{1,0:T(8,128)S(1)} %convolution_subtract_fusion.16), custom_call_target="Cholesky" | custom-call | tf_op jit(solution)/shard_map/jit(cholesky)/cholesky | solution.py:59
  141.5 10.3 %select_select_fusion.1 = f32[512,512]{1,0:T(8,128)S(1)} fusion(f32[512,512]{1,0:T(8,128)S(1)} %get-tuple-element.154, pred[]{:T(512)S(6)} %cholesky.348), kind=kLoop, calls=%fused_computation.25 | loop fusion | flops 1048576 | bytes 2097153 | tf_op jit(solution)/shard_map/triangular_solve/select.3 | solution.py:10
  151.9 8.0 while.16
  159.9 39.3 %custom-call.34 = f32[4,128,128]{1,2,0:T(8,128)S(1)} custom-call(f32[4,128,128]{2,1,0:T(8,128)S(1)} %get-tuple-element.75), custom_call_target="InvertDiagBlocksLowerTriangular" | custom-call | tf_op jit(solution)/shard_map/triangular_solve/custom-call.3 | solution.py:10
  215.2 11.7 %cholesky.358 = f32[128,128]{1,0:T(8,128)S(1)} custom-call(f32[128,128]{1,0:T(8,128)S(1)} %cholesky.439), custom_call_target="Cholesky" | custom-call | tf_op jit(solution)/shard_map/jit(cholesky)/cholesky | solution.py:64
  227.1 10.2 %custom-call.35 = f32[1,128,128]{1,2,0:T(8,128)S(1)} custom-call(f32[1,128,128]{2,1,0:T(8,128)S(1)} %get-tuple-element.152), custom_call_target="InvertDiagBlocksLowerTriangular" | custom-call | tf_op jit(solution)/shard_map/jit(cholesky)/cholesky | solution.py:64
  239.8 11.7 %cholesky.377 = f32[128,128]{1,0:T(8,128)S(1)} custom-call(f32[128,128]{1,0:T(8,128)S(1)} %cholesky.443), custom_call_target="Cholesky" | custom-call | tf_op jit(solution)/shard_map/jit(cholesky)/cholesky | solution.py:64
  252.9 9.8 %custom-call.36 = f32[1,128,128]{1,2,0:T(8,128)S(1)} custom-call(f32[1,128,128]{2,1,0:T(8,128)S(1)} %get-tuple-element.149), custom_call_target="InvertDiagBlocksLowerTriangular" | custom-call | tf_op jit(solution)/shard_map/jit(cholesky)/cholesky | solution.py:64
  265.9 13.2 %cholesky.398 = f32[128,128]{1,0:T(8,128)} custom-call(f32[128,128]{1,0:T(8,128)} %cholesky.448), custom_call_target="Cholesky" | custom-call | tf_op jit(solution)/shard_map/jit(cholesky)/cholesky | solution.py:64
  281.3 11.3 %custom-call.37 = f32[1,128,128]{1,2,0:T(8,128)} custom-call(f32[1,128,128]{2,1,0:T(8,128)} %get-tuple-element.146), custom_call_target="InvertDiagBlocksLowerTriangular" | custom-call | tf_op jit(solution)/shard_map/jit(cholesky)/cholesky | solution.py:64
  294.9 11.7 %cholesky.415 = f32[128,128]{1,0:T(8,128)S(1)} custom-call(f32[128,128]{1,0:T(8,128)S(1)} %convolution_subtract_fusion.15), custom_call_target="Cholesky" | custom-call | tf_op jit(solution)/shard_map/jit(cholesky)/cholesky | solution.py:64
  310.8 11.6 %while.17 = (s32[]{:T(128)}, f32[512,512]{1,0:T(8,128)}, s32[4,2]{0,1:T(2,128)S(1)}, f32[4,128,128]{2,1,0:T(8,128)S(1)}, s32[]{:T(128)}) while((s32[]{:T(128)}, f32[512,512]{1,0:T(8,128)}, s32[4,2]{0,1:T(2,128)S(1)}, f32[4,128,128]{2,1,0:T(8,128)S(1)}, s32[]{:T(128)}) %tuple.108), condition=%wide.while_cond.clone, body=%wide.while_body.clone.sunk | while | flops 2 | bytes 131181 | solution.py:10
  322.5 39.9 %custom-call.38 = f32[4,128,128]{1,2,0:T(8,128)} custom-call(f32[4,128,128]{2,1,0:T(8,128)S(1)} %get-tuple-element.76), custom_call_target="InvertDiagBlocksLowerTriangular" | custom-call | tf_op jit(solution)/shard_map/triangular_solve/custom-call.3 | solution.py:10
  384.6 24.9 %all-gather.18.cloned.1.call-done = f32[2048,512]{0,1:T(8,128)} async-done(((f32[256,512]{0,1:T(8,128)}), f32[2048,512]{0,1:T(8,128)}) %all-gather.18.cloned.1.call-update) | async-done | bytes 4194320 | tf_op jit(solution)/shard_map/all_gather | solution.py:69
  409.5 5.5 copy.34
  415.0 28.0 %all-gather.14.cloned.1.call-done = f32[2048,512]{0,1:T(8,128)} async-done(((f32[256,512]{0,1:T(8,128)}), f32[2048,512]{0,1:T(8,128)}) %all-gather.14.cloned.1.call-update) | async-done | bytes 4194320 | tf_op jit(solution)/shard_map/all_gather | solution.py:68
  443.1 5.4 copy.32
  448.4 73.9 %all-gather.20.cloned.1.call-done = f32[4096,512]{0,1:T(8,128)} async-done(((f32[256,512]{0,1:T(8,128)}), f32[4096,512]{0,1:T(8,128)}) %all-gather.20.cloned.1.call-update) | async-done | bytes 8388624 | tf_op jit(solution)/shard_map/all_gather | solution.py:73
  522.4 9.0 copy.35
  531.4 69.8 %all-gather.16.cloned.1.call-done = f32[4096,512]{0,1:T(8,128)} async-done(((f32[256,512]{0,1:T(8,128)}), f32[4096,512]{0,1:T(8,128)}) %all-gather.16.cloned.1.call-update) | async-done | bytes 8388624 | tf_op jit(solution)/shard_map/all_gather | solution.py:72
  601.1 9.0 copy.33
  610.1 305.6 %while.15 = (s32[]{:T(128)}, f32[8,16,128,128]{3,2,1,0:T(8,128)}, f32[8,16,128,128]{3,2,1,0:T(8,128)}, s32[8,16]{1,0:T(8,128)S(1)}, f32[16,128,512]{2,1,0:T(8,12...) while((s32[]{:T(128)}, f32[8,16,128,128]{3,2,1,0:T(8,128)}, ...), condition=%wide.region_9.12_spmd, body=%wide.region_8.11_spmd.sunk | while | flops 3221751808 | bytes 54535400 | solution.py:44
  610.1 4.9 gather_fusion
  615.1 6.2 gather_fusion.1
  621.2 7.4 fusion.128
  628.6 4.9 gather_fusion.2
  633.6 6.2 gather_fusion.3
  639.7 8.6 fusion.129
  653.3 6.2 gather_fusion.1
  659.4 7.4 fusion.128
  666.8 4.9 gather_fusion.2
  671.8 6.2 gather_fusion.3
  677.9 8.6 fusion.129
  691.4 6.2 gather_fusion.1
  697.6 7.4 fusion.128
  709.9 6.2 gather_fusion.3
  716.1 8.6 fusion.129
  729.6 6.2 gather_fusion.1
  735.8 7.4 fusion.128
  748.1 6.2 gather_fusion.3
  754.3 8.6 fusion.129
  767.8 6.2 gather_fusion.1
  774.0 7.4 fusion.128
  786.3 6.2 gather_fusion.3
  792.5 8.6 fusion.129
  806.0 6.2 gather_fusion.1
  812.2 7.4 fusion.128
  824.5 6.2 gather_fusion.3
  830.7 8.6 fusion.129
  844.2 6.2 gather_fusion.1
  850.4 7.4 fusion.128
  862.7 6.2 gather_fusion.3
  868.9 8.6 fusion.129
  882.4 6.2 gather_fusion.1
  888.6 7.4 fusion.128
  900.9 6.2 gather_fusion.3
  907.1 8.6 fusion.129
  (176 shorter events, 144.1 us)
Async XLA Ops:
  7.2 48.1 %all-gather.8.cloned.1.call-start = ((), (), s32[]{:S(2)}) async-start(), calls=%async_computation | async-start | bytes 1114112 | tf_op jit(solution)/shard_map/all_gather | solution.py:55
  7.9 191.4 %all-gather.12.cloned.1.call-start = ((), (), s32[]{:S(2)}) async-start(), calls=%async_computation.2 | async-start | bytes 1114112 | tf_op jit(solution)/shard_map/all_gather | solution.py:56
  8.6 200.2 %all-gather.10.cloned.1.call-start = ((), (), s32[]{:S(2)}) async-start(), calls=%async_computation.1 | async-start | bytes 1114112 | tf_op jit(solution)/shard_map/all_gather | solution.py:57
  9.4 400.1 %all-gather.18.cloned.1.call-start = ((), (), s32[]{:S(2)}) async-start(), calls=%async_computation.5 | async-start | bytes 4718592 | tf_op jit(solution)/shard_map/all_gather | solution.py:69
  199.2 9.6 %copy-start.5 = (f32[4,128,128]{1,2,0:T(8,128)}, f32[4,128,128]{1,2,0:T(8,128)S(1)}, u32[]{:S(2)}) copy-start(f32[4,128,128]{1,2,0:T(8,128)S(1)} %custom-call.34) | copy-start | bytes 786436
  202.7 2.5 copy-start
  205.2 2.5 copy-start.3
  214.2 1.0 copy-start.2
  215.2 147.3 %copy-start.6 = (f32[4,128,128]{1,2,0:T(8,128)S(1)}, f32[4,128,128]{1,2,0:T(8,128)}, u32[]{:S(2)}) copy-start(f32[4,128,128]{1,2,0:T(8,128)} %copy-done.5) | copy-start | bytes 786436
  239.8 22.9 %copy-start.8 = (f32[384,128]{1,0:T(8,128)}, f32[384,128]{1,0:T(8,128)S(1)}, u32[]{:S(2)}) copy-start(f32[384,128]{1,0:T(8,128)S(1)} %convolution_subtract_fusion.5) | copy-start | bytes 589828
  262.7 106.5 %copy-start.1 = (f32[512,128]{0,1:T(8,128)S(1)}, f32[512,128]{0,1:T(8,128)}, u32[]{:S(2)}) copy-start(f32[512,128]{0,1:T(8,128)} %copy-done) | copy-start | bytes 786436
  262.7 106.5 %copy-start.4 = (f32[512,128]{0,1:T(8,128)S(1)}, f32[512,128]{0,1:T(8,128)}, u32[]{:S(2)}) copy-start(f32[512,128]{0,1:T(8,128)} %copy-done.3) | copy-start | bytes 786436
  262.7 106.5 %copy-start.7 = (f32[512,128]{0,1:T(8,128)S(1)}, f32[512,128]{0,1:T(8,128)}, u32[]{:S(2)}) copy-start(f32[512,128]{0,1:T(8,128)} %fusion.75) | copy-start | bytes 786436
  362.4 8.9 copy-start.9
  371.4 8.9 copy-start.10
  378.0 65.0 %all-gather.14.cloned.1.call-start = ((), (), s32[]{:S(2)}) async-start(), calls=%async_computation.3 | async-start | bytes 4718592 | tf_op jit(solution)/shard_map/all_gather | solution.py:68
  378.9 143.4 %all-gather.20.cloned.1.call-start = ((), (), s32[]{:S(2)}) async-start(), calls=%async_computation.6 | async-start | bytes 8912896 | tf_op jit(solution)/shard_map/all_gather | solution.py:73
  379.5 221.6 %all-gather.16.cloned.1.call-start = ((), (), s32[]{:S(2)}) async-start(), calls=%async_computation.4 | async-start | bytes 8912896 | tf_op jit(solution)/shard_map/all_gather | solution.py:72
Sparse Core Ops, SparseCore 0:
  10.1 45.0 all-gather.7
  57.4 42.2 all-gather.11
  101.8 42.5 all-gather.9
  378.1 31.3 all-gather.17
  411.0 31.9 all-gather.13
  445.0 77.2 all-gather.19
  524.5 76.6 all-gather.15
where the time goes:
time: 934 us; the launch traced here: 923 us
  other arithmetic  257 us (28%)
  waiting for transfers between devices  246 us (26%)
  local copies, waits for them, and re-layouts  235 us (25%)
  matrix products  164 us (18%)
  between operations  20.2 us (2%)
    another operation x7, other arithmetic, apply_solve(): lax.linalg.triangular_solve(chol, rows, left_side=False, lower=True, tran...  92.4 us
    another operation x15, other arithmetic, shards(): chol_two = jnp.linalg.cholesky(schur)  83.8 us
    another operation x14, other arithmetic, shards(): chol_one = jnp.linalg.cholesky(full_one)  78.6 us
    all_gather x1, waiting for transfers between devices, shards(): lax.all_gather(lower_two, 'row', axis=0, tiled=True)  73.9 us
    all_gather x1, waiting for transfers between devices, shards(): lax.all_gather(lower_one, 'row', axis=0, tiled=True)  69.8 us
    dot_general x8, matrix products, one_group(): jnp.einsum('kaw,kbw->kab', row_blocks_two[row_id], col_blocks_two[col_id]...  68.7 us
    dot_general x8, matrix products, one_group(): jnp.einsum('kaw,kbw->kab', row_blocks_one[row_id], col_blocks_one[col_id]...  59.2 us
    gather x8, local copies, waits for them, and re-layouts, one_group(): col_blocks_one[col_id]  49.3 us
  transfers between devices with their start and end apart: 7, of which 5 were waited for; matrix products, arithmetic and copies ran while one was open for 19% of the time, Pallas kernels for 0%

commit v1 on v0

--- a/solution.py
+++ b/solution.py
@@ -2,6 +2,19 @@
 import jax.numpy as jnp
 from jax import lax
 from jax.sharding import PartitionSpec as P
+
+
+def ring_gather(x, axis, dim):
+    ways = lax.axis_size(axis)
+    up = [(d, (d + 1) % ways) for d in range(ways)]
+    down = [(d, (d - 1) % ways) for d in range(ways)]
+    earlier, later = ([x], [x])
+    for _ in range(ways // 2):
+        earlier.append(lax.ppermute(earlier[-1], axis, up))
+    for _ in range((ways - 1) // 2):
+        later.append(lax.ppermute(later[-1], axis, down))
+    line = jnp.concatenate([*earlier[::-1], *later[1:]], axis=dim)
+    return jnp.roll(line, (lax.axis_index(axis) - ways // 2) * x.shape[dim], axis=dim)
 
 
 def make_solver(chol):
@@ -69,7 +82,7 @@
         lax.all_gather(lower_two, "col", axis=0, tiled=True),
     )
     col_one, col_two = (
-        lax.all_gather(lower_one, "row", axis=0, tiled=True),
+        ring_gather(lower_one, "row", 0),
         lax.all_gather(lower_two, "row", axis=0, tiled=True),
     )
     updated = pair_updates(targets, pattern, row_one, row_two, col_one, col_two, shard_blocks)

time: 934 us -> 858 us (0.919)
  waiting for transfers between devices: 246 us -> 122 us
  starting transfers between devices: 0.27 us -> 39.7 us
  local copies, waits for them, and re-layouts: 235 us -> 253 us
  other arithmetic: 257 us -> 242 us
  between operations: 20.2 us -> 30.6 us
    all_gather x1, waiting for transfers between devices: 73.9 us -> 3.24 us  [shards(): lax.all_gather(lower_two, 'row', axis=0, tiled=True)]
    ppermute x0 -> x15, waiting for transfers between devices: none -> 70 us  [the longest x8 62.7 us: ring_gather(): earlier.append(lax.ppermute(earlier[-1], axis, up))]
    all_gather x1 -> x0, waiting for transfers between devices: 69.8 us -> none  [shards(): lax.all_gather(lower_one, 'row', axis=0, tiled=True)]
    ppermute x0 -> x15, starting transfers between devices: none -> 39.5 us  [the longest x7 38.2 us: ring_gather(): later.append(lax.ppermute(later[-1], axis, down))]
    all_gather x1, waiting for transfers between devices: 28 us -> 0.01 us  [shards(): lax.all_gather(lower_one, 'col', axis=0, tiled=True)]
    all_gather x1, waiting for transfers between devices: 24.9 us -> 0.01 us  [shards(): lax.all_gather(lower_two, 'col', axis=0, tiled=True)]
    unnamed x24 -> x59, local copies, waits for them, and re-layouts: 5.08 us -> 22.1 us
    dynamic_slice x0 -> x2, local copies, waits for them, and re-layouts: none -> 13.1 us  [ring_gather(): jnp.roll(line, (lax.axis_index(axis) - ways // 2) * x.shape[dim], axis=dim)]
  transfers between devices with their start and end apart: 7 -> 21, of which waited for: 5 -> 11; matrix products, arithmetic and copies ran while one was open for 19% -> 23% of each run, Pallas kernels for 0% -> 0%
where the time goes in v1:
time: 858 us; the launch traced here: 846 us
  local copies, waits for them, and re-layouts  253 us (29%)
  other arithmetic  242 us (28%)
  matrix products  159 us (19%)
  waiting for transfers between devices  122 us (14%)
  starting transfers between devices  39.7 us (5%)
  between operations  30.6 us (4%)
    another operation x7, other arithmetic, apply_solve(): lax.linalg.triangular_solve(chol, rows, left_side=False, lower=True, tran...  80.8 us
    another operation x15, other arithmetic, shards(): chol_two = jnp.linalg.cholesky(schur)  79.5 us
    another operation x14, other arithmetic, shards(): chol_one = jnp.linalg.cholesky(full_one)  78.6 us
    dot_general x8, matrix products, one_group(): jnp.einsum('kaw,kbw->kab', row_blocks_two[row_id], col_blocks_two[col_id]...  68.7 us
    ppermute x8, waiting for transfers between devices, ring_gather(): earlier.append(lax.ppermute(earlier[-1], axis, up))  62.7 us
    dot_general x8, matrix products, one_group(): jnp.einsum('kaw,kbw->kab', row_blocks_one[row_id], col_blocks_one[col_id]...  59.2 us
    gather x8, local copies, waits for them, and re-layouts, one_group(): col_blocks_one[col_id]  49.2 us
    gather x8, local copies, waits for them, and re-layouts, one_group(): col_blocks_two[col_id]  49.2 us
  transfers between devices with their start and end apart: 21, of which 11 were waited for; matrix products, arithmetic and copies ran while one was open for 23% of the time, Pallas kernels for 0%

profile of v1, /device:TPU:0, one launch (start us, length us, event | category | flops | bytes accessed | tf_op | source)
XLA Modules:
  0.0 846.0 jit_solution(13828524152370914763)
XLA Ops:
  9.4 45.8 %all-gather.7.cloned.1.call-done = f32[512,512]{1,0:T(8,128)} async-done(((f32[32,512]{1,0:T(8,128)}), f32[512,512]{1,0:T(8,128)}) %all-gather.7.cloned.1.call-update) | async-done | bytes 1048592 | tf_op jit(solution)/shard_map/all_gather | solution.py:68
  58.3 11.7 %cholesky.286 = f32[128,128]{1,0:T(8,128)S(1)} custom-call(f32[128,128]{1,0:T(8,128)S(1)} %cholesky.426), custom_call_target="Cholesky" | custom-call | tf_op jit(solution)/shard_map/jit(cholesky)/cholesky | solution.py:72
  70.0 9.8 %custom-call.31 = f32[1,128,128]{1,2,0:T(8,128)S(1)} custom-call(f32[1,128,128]{2,1,0:T(8,128)S(1)} %get-tuple-element.174), custom_call_target="InvertDiagBlocksLowerTriangular" | custom-call | tf_op jit(solution)/shard_map/jit(cholesky)/cholesky | solution.py:72
  80.7 11.7 %cholesky.305 = f32[128,128]{1,0:T(8,128)S(1)} custom-call(f32[128,128]{1,0:T(8,128)S(1)} %cholesky.430), custom_call_target="Cholesky" | custom-call | tf_op jit(solution)/shard_map/jit(cholesky)/cholesky | solution.py:72
  92.4 10.0 %custom-call.32 = f32[1,128,128]{1,2,0:T(8,128)S(1)} custom-call(f32[1,128,128]{2,1,0:T(8,128)S(1)} %get-tuple-element.171), custom_call_target="InvertDiagBlocksLowerTriangular" | custom-call | tf_op jit(solution)/shard_map/jit(cholesky)/cholesky | solution.py:72
  103.1 11.7 %cholesky.326 = f32[128,128]{1,0:T(8,128)S(1)} custom-call(f32[128,128]{1,0:T(8,128)S(1)} %cholesky.435), custom_call_target="Cholesky" | custom-call | tf_op jit(solution)/shard_map/jit(cholesky)/cholesky | solution.py:72
  115.5 9.8 %custom-call.33 = f32[1,128,128]{1,2,0:T(8,128)S(1)} custom-call(f32[1,128,128]{2,1,0:T(8,128)S(1)} %get-tuple-element.168), custom_call_target="InvertDiagBlocksLowerTriangular" | custom-call | tf_op jit(solution)/shard_map/jit(cholesky)/cholesky | solution.py:72
  125.9 11.7 %cholesky.343 = f32[128,128]{1,0:T(8,128)S(1)} custom-call(f32[128,128]{1,0:T(8,128)S(1)} %convolution_subtract_fusion.16), custom_call_target="Cholesky" | custom-call | tf_op jit(solution)/shard_map/jit(cholesky)/cholesky | solution.py:72
  151.8 8.0 while.16
  159.8 39.3 %custom-call.34 = f32[4,128,128]{1,2,0:T(8,128)S(1)} custom-call(f32[4,128,128]{2,1,0:T(8,128)S(1)} %get-tuple-element.75), custom_call_target="InvertDiagBlocksLowerTriangular" | custom-call | tf_op jit(solution)/shard_map/triangular_solve/custom-call.3 | solution.py:23
  221.3 12.1 %cholesky.358 = f32[128,128]{1,0:T(8,128)S(1)} custom-call(f32[128,128]{1,0:T(8,128)S(1)} %cholesky.439), custom_call_target="Cholesky" | custom-call | tf_op jit(solution)/shard_map/jit(cholesky)/cholesky | solution.py:77
  233.5 9.8 %custom-call.35 = f32[1,128,128]{1,2,0:T(8,128)S(1)} custom-call(f32[1,128,128]{2,1,0:T(8,128)S(1)} %get-tuple-element.164), custom_call_target="InvertDiagBlocksLowerTriangular" | custom-call | tf_op jit(solution)/shard_map/jit(cholesky)/cholesky | solution.py:77
  245.9 11.7 %cholesky.377 = f32[128,128]{1,0:T(8,128)S(1)} custom-call(f32[128,128]{1,0:T(8,128)S(1)} %cholesky.443), custom_call_target="Cholesky" | custom-call | tf_op jit(solution)/shard_map/jit(cholesky)/cholesky | solution.py:77
  258.9 9.8 %custom-call.36 = f32[1,128,128]{1,2,0:T(8,128)S(1)} custom-call(f32[1,128,128]{2,1,0:T(8,128)S(1)} %get-tuple-element.161), custom_call_target="InvertDiagBlocksLowerTriangular" | custom-call | tf_op jit(solution)/shard_map/jit(cholesky)/cholesky | solution.py:77
  270.3 11.9 %cholesky.398 = f32[128,128]{1,0:T(8,128)S(1)} custom-call(f32[128,128]{1,0:T(8,128)S(1)} %cholesky.448), custom_call_target="Cholesky" | custom-call | tf_op jit(solution)/shard_map/jit(cholesky)/cholesky | solution.py:77
  282.8 9.8 %custom-call.37 = f32[1,128,128]{1,2,0:T(8,128)S(1)} custom-call(f32[1,128,128]{2,1,0:T(8,128)S(1)} %get-tuple-element.158), custom_call_target="InvertDiagBlocksLowerTriangular" | custom-call | tf_op jit(solution)/shard_map/jit(cholesky)/cholesky | solution.py:77
  294.1 11.7 %cholesky.415 = f32[128,128]{1,0:T(8,128)S(1)} custom-call(f32[128,128]{1,0:T(8,128)S(1)} %convolution_subtract_fusion.15), custom_call_target="Cholesky" | custom-call | tf_op jit(solution)/shard_map/jit(cholesky)/cholesky | solution.py:77
  309.1 8.0 while.17
  317.2 39.5 %custom-call.38 = f32[4,128,128]{1,2,0:T(8,128)S(1)} custom-call(f32[4,128,128]{2,1,0:T(8,128)S(1)} %get-tuple-element.76), custom_call_target="InvertDiagBlocksLowerTriangular" | custom-call | tf_op jit(solution)/shard_map/triangular_solve/custom-call.3 | solution.py:23
  365.7 14.2 %collective-permute-done = f32[256,512]{0,1:T(8,128)S(1)} collective-permute-done((f32[256,512]{0,1:T(8,128)}, f32[256,512]{0,1:T(8,128)S(1)}, u32[]{:S(2)}, u32[]{:S(2)}) %collective-permute-start) | collective-permute-done | bytes 524320 | tf_op jit(solution)/shard_map/ppermute | solution.py:13
  385.2 9.0 %collective-permute-done.1 = f32[256,512]{0,1:T(8,128)S(1)} collective-permute-done((f32[256,512]{0,1:T(8,128)S(1)}, f32[256,512]{0,1:T(8,128)S(1)}, u32[]{:S(2)}, u32[]{:S(2)}) %collective-permute-start.1) | collective-permute-done | bytes 524320 | tf_op jit(solution)/shard_map/ppermute | solution.py:13
  399.6 8.1 collective-permute-done.2
  413.1 7.3 collective-permute-done.3
  426.5 7.0 collective-permute-done.4
  434.3 5.6 collective-permute-start.12
  439.9 9.3 %collective-permute-done.5 = f32[256,512]{0,1:T(8,128)S(1)} collective-permute-done((f32[256,512]{0,1:T(8,128)S(1)}, f32[256,512]{0,1:T(8,128)S(1)}, u32[]{:S(2)}, u32[]{:S(2)}) %collective-permute-start.5) | collective-permute-done | bytes 524320 | tf_op jit(solution)/shard_map/ppermute | solution.py:13
  449.2 7.3 collective-permute-done.12
  456.6 5.9 collective-permute-start.13
  500.4 9.3 %copy.35 = f32[4096,512]{1,0:T(8,128)} copy(f32[4096,512]{0,1:T(8,128)} %constant_dynamic-slice_fusion.4) | data formatting | bytes 16777216 | tf_op jit(solution)/shard_map/jit(_roll_dynamic)/dynamic_slice | solution.py:17
  509.7 5.5 copy.43
  523.8 9.0 %copy.44 = f32[4096,512]{1,0:T(8,128)} copy(f32[4096,512]{0,1:T(8,128)} %all-gather.17.cloned.1.call-done) | data formatting | bytes 16777216 | tf_op jit(solution)/shard_map/while | solution.py:57
  532.8 305.8 %while.15 = (s32[]{:T(128)}, f32[8,16,128,128]{3,2,1,0:T(8,128)}, f32[8,16,128,128]{3,2,1,0:T(8,128)}, s32[8,16]{1,0:T(8,128)S(1)}, f32[16,128,512]{2,1,0:T(8,12...) while((s32[]{:T(128)}, f32[8,16,128,128]{3,2,1,0:T(8,128)}, ...), condition=%wide.region_9.12_spmd, body=%wide.region_8.11_spmd.sunk | while | flops 3221751808 | bytes 54535400 | solution.py:57
  537.8 6.1 gather_fusion.1
  544.0 7.4 fusion.128
  556.4 6.1 gather_fusion.3
  562.5 8.6 %fusion.129 = f32[8,16,128,128]{3,2,1,0:T(8,128)} fusion(f32[8,16,128,128]{3,2,1,0:T(8,128)} %get-tuple-element.341, s32[]{:T(128)} %get-tuple-element.340, f32[16,128,128]{2,1,0:T(8,128)S(1)} %fusion.128, f32[16,128,512]{2,1,0:T(8,128)} %gather_fusion.2, f32[16,128,512]{2,1,0:T(8,128)} %gather_fusion.3, f32[8,16,128,128]{3,2,1,0:T(8,128)} %get-tuple-element.352), kind=kOutput, calls=%fused_computation.11.clone.1 | convolution fusion | flops 1611137024 | bytes 11534848 | tf_op jit(solution)/shard_map/while/body/eval_jaxpr/kaw,kbw->kab/dot_general | solution.py:52
  576.1 6.1 gather_fusion.1
  582.2 7.4 fusion.128
  594.6 6.1 gather_fusion.3
  600.7 8.6 %fusion.129 = f32[8,16,128,128]{3,2,1,0:T(8,128)} fusion(f32[8,16,128,128]{3,2,1,0:T(8,128)} %get-tuple-element.341, s32[]{:T(128)} %get-tuple-element.340, f32[16,128,128]{2,1,0:T(8,128)S(1)} %fusion.128, f32[16,128,512]{2,1,0:T(8,128)} %gather_fusion.2, f32[16,128,512]{2,1,0:T(8,128)} %gather_fusion.3, f32[8,16,128,128]{3,2,1,0:T(8,128)} %get-tuple-element.352), kind=kOutput, calls=%fused_computation.11.clone.1 | convolution fusion | flops 1611137024 | bytes 11534848 | tf_op jit(solution)/shard_map/while/body/eval_jaxpr/kaw,kbw->kab/dot_general | solution.py:52
  614.3 6.1 gather_fusion.1
  620.4 7.4 fusion.128
  632.8 6.1 gather_fusion.3
  639.0 8.6 %fusion.129 = f32[8,16,128,128]{3,2,1,0:T(8,128)} fusion(f32[8,16,128,128]{3,2,1,0:T(8,128)} %get-tuple-element.341, s32[]{:T(128)} %get-tuple-element.340, f32[16,128,128]{2,1,0:T(8,128)S(1)} %fusion.128, f32[16,128,512]{2,1,0:T(8,128)} %gather_fusion.2, f32[16,128,512]{2,1,0:T(8,128)} %gather_fusion.3, f32[8,16,128,128]{3,2,1,0:T(8,128)} %get-tuple-element.352), kind=kOutput, calls=%fused_computation.11.clone.1 | convolution fusion | flops 1611137024 | bytes 11534848 | tf_op jit(solution)/shard_map/while/body/eval_jaxpr/kaw,kbw->kab/dot_general | solution.py:52
  652.5 6.1 gather_fusion.1
  658.7 7.4 fusion.128
  671.0 6.1 gather_fusion.3
  677.2 8.6 %fusion.129 = f32[8,16,128,128]{3,2,1,0:T(8,128)} fusion(f32[8,16,128,128]{3,2,1,0:T(8,128)} %get-tuple-element.341, s32[]{:T(128)} %get-tuple-element.340, f32[16,128,128]{2,1,0:T(8,128)S(1)} %fusion.128, f32[16,128,512]{2,1,0:T(8,128)} %gather_fusion.2, f32[16,128,512]{2,1,0:T(8,128)} %gather_fusion.3, f32[8,16,128,128]{3,2,1,0:T(8,128)} %get-tuple-element.352), kind=kOutput, calls=%fused_computation.11.clone.1 | convolution fusion | flops 1611137024 | bytes 11534848 | tf_op jit(solution)/shard_map/while/body/eval_jaxpr/kaw,kbw->kab/dot_general | solution.py:52
  690.8 6.1 gather_fusion.1
  696.9 7.4 fusion.128
  709.3 6.1 gather_fusion.3
  715.4 8.6 %fusion.129 = f32[8,16,128,128]{3,2,1,0:T(8,128)} fusion(f32[8,16,128,128]{3,2,1,0:T(8,128)} %get-tuple-element.341, s32[]{:T(128)} %get-tuple-element.340, f32[16,128,128]{2,1,0:T(8,128)S(1)} %fusion.128, f32[16,128,512]{2,1,0:T(8,128)} %gather_fusion.2, f32[16,128,512]{2,1,0:T(8,128)} %gather_fusion.3, f32[8,16,128,128]{3,2,1,0:T(8,128)} %get-tuple-element.352), kind=kOutput, calls=%fused_computation.11.clone.1 | convolution fusion | flops 1611137024 | bytes 11534848 | tf_op jit(solution)/shard_map/while/body/eval_jaxpr/kaw,kbw->kab/dot_general | solution.py:52
  729.0 6.1 gather_fusion.1
  735.1 7.4 fusion.128
  747.5 6.1 gather_fusion.3
  753.6 8.6 %fusion.129 = f32[8,16,128,128]{3,2,1,0:T(8,128)} fusion(f32[8,16,128,128]{3,2,1,0:T(8,128)} %get-tuple-element.341, s32[]{:T(128)} %get-tuple-element.340, f32[16,128,128]{2,1,0:T(8,128)S(1)} %fusion.128, f32[16,128,512]{2,1,0:T(8,128)} %gather_fusion.2, f32[16,128,512]{2,1,0:T(8,128)} %gather_fusion.3, f32[8,16,128,128]{3,2,1,0:T(8,128)} %get-tuple-element.352), kind=kOutput, calls=%fused_computation.11.clone.1 | convolution fusion | flops 1611137024 | bytes 11534848 | tf_op jit(solution)/shard_map/while/body/eval_jaxpr/kaw,kbw->kab/dot_general | solution.py:52
  767.2 6.1 gather_fusion.1
  773.4 7.4 fusion.128
  785.7 6.1 gather_fusion.3
  791.9 8.6 %fusion.129 = f32[8,16,128,128]{3,2,1,0:T(8,128)} fusion(f32[8,16,128,128]{3,2,1,0:T(8,128)} %get-tuple-element.341, s32[]{:T(128)} %get-tuple-element.340, f32[16,128,128]{2,1,0:T(8,128)S(1)} %fusion.128, f32[16,128,512]{2,1,0:T(8,128)} %gather_fusion.2, f32[16,128,512]{2,1,0:T(8,128)} %gather_fusion.3, f32[8,16,128,128]{3,2,1,0:T(8,128)} %get-tuple-element.352), kind=kOutput, calls=%fused_computation.11.clone.1 | convolution fusion | flops 1611137024 | bytes 11534848 | tf_op jit(solution)/shard_map/while/body/eval_jaxpr/kaw,kbw->kab/dot_general | solution.py:52
  805.4 6.1 gather_fusion.1
  811.6 7.4 fusion.128
  824.0 6.1 gather_fusion.3
  830.1 8.6 %fusion.129 = f32[8,16,128,128]{3,2,1,0:T(8,128)} fusion(f32[8,16,128,128]{3,2,1,0:T(8,128)} %get-tuple-element.341, s32[]{:T(128)} %get-tuple-element.340, f32[16,128,128]{2,1,0:T(8,128)S(1)} %fusion.128, f32[16,128,512]{2,1,0:T(8,128)} %gather_fusion.2, f32[16,128,512]{2,1,0:T(8,128)} %gather_fusion.3, f32[8,16,128,128]{3,2,1,0:T(8,128)} %get-tuple-element.352), kind=kOutput, calls=%fused_computation.11.clone.1 | convolution fusion | flops 1611137024 | bytes 11534848 | tf_op jit(solution)/shard_map/while/body/eval_jaxpr/kaw,kbw->kab/dot_general | solution.py:52
  (242 shorter events, 213.5 us)
Async XLA Ops:
  7.2 48.1 %all-gather.7.cloned.1.call-start = ((), (), s32[]{:S(2)}) async-start(), calls=%async_computation | async-start | bytes 1114112 | tf_op jit(solution)/shard_map/all_gather | solution.py:68
  7.9 198.0 %all-gather.11.cloned.1.call-start = ((), (), s32[]{:S(2)}) async-start(), calls=%async_computation.2 | async-start | bytes 1114112 | tf_op jit(solution)/shard_map/all_gather | solution.py:69
  8.6 206.6 %all-gather.9.cloned.1.call-start = ((), (), s32[]{:S(2)}) async-start(), calls=%async_computation.1 | async-start | bytes 1114112 | tf_op jit(solution)/shard_map/all_gather | solution.py:70
  9.4 500.4 %all-gather.15.cloned.1.call-start = ((), (), s32[]{:S(2)}) async-start(), calls=%async_computation.4 | async-start | bytes 4718592 | tf_op jit(solution)/shard_map/all_gather | solution.py:82
  205.9 157.9 %copy-start.11 = (f32[256,128]{0,1:T(8,128)}, f32[256,128]{0,1:T(8,128)S(1)}, u32[]{:S(2)}) copy-start(f32[256,128]{0,1:T(8,128)S(1)} %fusion.76) | copy-start | bytes 393220
  208.9 258.3 %copy-start.13 = (s32[128,2]{0,1:T(2,128)S(1)}, s32[128,2]{0,1:T(2,128)}, u32[]{:S(2)}) copy-start(s32[128,2]{0,1:T(2,128)} %param.18) | copy-start | bytes 3076
  220.3 1.0 copy-start
  362.9 152.3 %all-gather.13.cloned.1.call-start = ((), (), s32[]{:S(2)}) async-start(), calls=%async_computation.3 | async-start | bytes 4718592 | tf_op jit(solution)/shard_map/all_gather | solution.py:81
  363.8 130.2 %copy-start.12 = (f32[256,128]{0,1:T(8,128)S(1)}, f32[256,128]{0,1:T(8,128)}, u32[]{:S(2)}) copy-start(f32[256,128]{0,1:T(8,128)} %copy-done.11) | copy-start | bytes 393220
  363.8 160.0 %all-gather.17.cloned.1.call-start = ((), (), s32[]{:S(2)}) async-start(), calls=%async_computation.5 | async-start | bytes 8912896 | tf_op jit(solution)/shard_map/all_gather | solution.py:86
  364.4 15.5 %collective-permute-start = (f32[256,512]{0,1:T(8,128)}, f32[256,512]{0,1:T(8,128)S(1)}, u32[]{:S(2)}, u32[]{:S(2)}) collective-permute-start(f32[256,512]{0,1:T(8,128)} %pad_maximum_fusion.3), channel_id=1, source_target_pairs={{0,8},{8,16},{16,24},{24,32},{32,40},{40,48},{48,56},{56,64},{64,7... | collective-permute-start | bytes 1572872 | tf_op jit(solution)/shard_map/ppermute | solution.py:13
  379.9 14.3 %collective-permute-start.1 = (f32[256,512]{0,1:T(8,128)S(1)}, f32[256,512]{0,1:T(8,128)S(1)}, u32[]{:S(2)}, u32[]{:S(2)}) collective-permute-start(f32[256,512]{0,1:T(8,128)S(1)} %collective-permute-done), channel_id=1, source_target_pairs={{0,8},{8,16},{16,24},{24,32},{32,40},{40,48},{48,56},{56,64},{64,7... | collective-permute-start | bytes 1572872 | tf_op jit(solution)/shard_map/ppermute | solution.py:13
  379.9 14.3 %collective-permute-start.8 = (f32[256,512]{0,1:T(8,128)}, f32[256,512]{0,1:T(8,128)S(1)}, u32[]{:S(2)}, u32[]{:S(2)}) collective-permute-start(f32[256,512]{0,1:T(8,128)} %pad_maximum_fusion.3), channel_id=1, source_target_pairs={{0,120},{8,0},{16,8},{24,16},{32,24},{40,32},{48,40},{56,48},{64,5... | collective-permute-start | bytes 1572872 | tf_op jit(solution)/shard_map/ppermute | solution.py:15
  394.2 13.5 %collective-permute-start.2 = (f32[256,512]{0,1:T(8,128)S(1)}, f32[256,512]{0,1:T(8,128)S(1)}, u32[]{:S(2)}, u32[]{:S(2)}) collective-permute-start(f32[256,512]{0,1:T(8,128)S(1)} %collective-permute-done.1), channel_id=1, source_target_pairs={{0,8},{8,16},{16,24},{24,32},{32,40},{40,48},{48,56},{56,64},{64,7... | collective-permute-start | bytes 1572872 | tf_op jit(solution)/shard_map/ppermute | solution.py:13
  394.2 13.5 %collective-permute-start.9 = (f32[256,512]{0,1:T(8,128)S(1)}, f32[256,512]{0,1:T(8,128)S(1)}, u32[]{:S(2)}, u32[]{:S(2)}) collective-permute-start(f32[256,512]{0,1:T(8,128)S(1)} %collective-permute-done.8), channel_id=1, source_target_pairs={{0,120},{8,0},{16,8},{24,16},{32,24},{40,32},{48,40},{56,48},{64,5... | collective-permute-start | bytes 1572872 | tf_op jit(solution)/shard_map/ppermute | solution.py:15
  407.7 12.6 %collective-permute-start.3 = (f32[256,512]{0,1:T(8,128)S(1)}, f32[256,512]{0,1:T(8,128)S(1)}, u32[]{:S(2)}, u32[]{:S(2)}) collective-permute-start(f32[256,512]{0,1:T(8,128)S(1)} %collective-permute-done.2), channel_id=1, source_target_pairs={{0,8},{8,16},{16,24},{24,32},{32,40},{40,48},{48,56},{56,64},{64,7... | collective-permute-start | bytes 1572872 | tf_op jit(solution)/shard_map/ppermute | solution.py:13
  407.7 12.6 %collective-permute-start.10 = (f32[256,512]{0,1:T(8,128)S(1)}, f32[256,512]{0,1:T(8,128)S(1)}, u32[]{:S(2)}, u32[]{:S(2)}) collective-permute-start(f32[256,512]{0,1:T(8,128)S(1)} %collective-permute-done.9), channel_id=1, source_target_pairs={{0,120},{8,0},{16,8},{24,16},{32,24},{40,32},{48,40},{56,48},{64,5... | collective-permute-start | bytes 1572872 | tf_op jit(solution)/shard_map/ppermute | solution.py:15
  420.3 36.2 %copy-start.5 = (f32[256,512]{0,1:T(8,128)}, f32[256,512]{0,1:T(8,128)S(1)}, u32[]{:S(2)}) copy-start(f32[256,512]{0,1:T(8,128)S(1)} %collective-permute-done.3) | copy-start | bytes 1572868
  420.3 13.1 %collective-permute-start.4 = (f32[256,512]{0,1:T(8,128)S(1)}, f32[256,512]{0,1:T(8,128)S(1)}, u32[]{:S(2)}, u32[]{:S(2)}) collective-permute-start(f32[256,512]{0,1:T(8,128)S(1)} %collective-permute-done.3), channel_id=1, source_target_pairs={{0,8},{8,16},{16,24},{24,32},{32,40},{40,48},{48,56},{56,64},{64,7... | collective-permute-start | bytes 1572872 | tf_op jit(solution)/shard_map/ppermute | solution.py:13
  420.4 0.8 copy-start.1
  421.2 12.3 %collective-permute-start.11 = (f32[256,512]{0,1:T(8,128)S(1)}, f32[256,512]{0,1:T(8,128)S(1)}, u32[]{:S(2)}, u32[]{:S(2)}) collective-permute-start(f32[256,512]{0,1:T(8,128)S(1)} %collective-permute-done.10), channel_id=1, source_target_pairs={{0,120},{8,0},{16,8},{24,16},{32,24},{40,32},{48,40},{56,48},{64,5... | collective-permute-start | bytes 1572872 | tf_op jit(solution)/shard_map/ppermute | solution.py:15
  433.5 29.0 %copy-start.7 = (f32[256,512]{0,1:T(8,128)}, f32[256,512]{0,1:T(8,128)S(1)}, u32[]{:S(2)}) copy-start(f32[256,512]{0,1:T(8,128)S(1)} %collective-permute-done.4) | copy-start | bytes 1572868
  433.5 15.8 %collective-permute-start.5 = (f32[256,512]{0,1:T(8,128)S(1)}, f32[256,512]{0,1:T(8,128)S(1)}, u32[]{:S(2)}, u32[]{:S(2)}) collective-permute-start(f32[256,512]{0,1:T(8,128)S(1)} %collective-permute-done.4), channel_id=1, source_target_pairs={{0,8},{8,16},{16,24},{24,32},{32,40},{40,48},{48,56},{56,64},{64,7... | collective-permute-start | bytes 1572872 | tf_op jit(solution)/shard_map/ppermute | solution.py:13
  433.5 0.9 copy-start.3
  434.3 22.2 %collective-permute-start.12 = (f32[256,512]{0,1:T(8,128)S(1)}, f32[256,512]{0,1:T(8,128)}, u32[]{:S(2)}, u32[]{:S(2)}) collective-permute-start(f32[256,512]{0,1:T(8,128)S(1)} %collective-permute-done.11), channel_id=1, source_target_pairs={{0,120},{8,0},{16,8},{24,16},{32,24},{40,32},{48,40},{56,48},{64,5... | collective-permute-start | bytes 1572872 | tf_op jit(solution)/shard_map/ppermute | solution.py:15
  449.2 17.9 %copy-start.9 = (f32[256,512]{0,1:T(8,128)}, f32[256,512]{0,1:T(8,128)S(1)}, u32[]{:S(2)}) copy-start(f32[256,512]{0,1:T(8,128)S(1)} %collective-permute-done.5) | copy-start | bytes 1572868
  449.2 17.9 %collective-permute-start.6 = (f32[256,512]{0,1:T(8,128)S(1)}, f32[256,512]{0,1:T(8,128)}, u32[]{:S(2)}, u32[]{:S(2)}) collective-permute-start(f32[256,512]{0,1:T(8,128)S(1)} %collective-permute-done.5), channel_id=1, source_target_pairs={{0,8},{8,16},{16,24},{24,32},{32,40},{40,48},{48,56},{56,64},{64,7... | collective-permute-start | bytes 1572872 | tf_op jit(solution)/shard_map/ppermute | solution.py:13
  456.6 14.9 %collective-permute-start.13 = (f32[256,512]{0,1:T(8,128)}, f32[256,512]{0,1:T(8,128)}, u32[]{:S(2)}, u32[]{:S(2)}) collective-permute-start(f32[256,512]{0,1:T(8,128)} %collective-permute-done.12), channel_id=1, source_target_pairs={{0,120},{8,0},{16,8},{24,16},{32,24},{40,32},{48,40},{56,48},{64,5... | collective-permute-start | bytes 1572872 | tf_op jit(solution)/shard_map/ppermute | solution.py:15
  467.1 12.8 %collective-permute-start.7 = (f32[256,512]{0,1:T(8,128)}, f32[256,512]{0,1:T(8,128)}, u32[]{:S(2)}, u32[]{:S(2)}) collective-permute-start(f32[256,512]{0,1:T(8,128)} %collective-permute-done.6), channel_id=1, source_target_pairs={{0,8},{8,16},{16,24},{24,32},{32,40},{40,48},{48,56},{56,64},{64,7... | collective-permute-start | bytes 1572872 | tf_op jit(solution)/shard_map/ppermute | solution.py:13
  471.4 22.2 %copy-start.10 = (f32[256,512]{0,1:T(8,128)S(1)}, f32[256,512]{0,1:T(8,128)}, u32[]{:S(2)}) copy-start(f32[256,512]{0,1:T(8,128)} %copy-done.9) | copy-start | bytes 1572868
  471.4 22.2 %copy-start.8 = (f32[256,512]{0,1:T(8,128)S(1)}, f32[256,512]{0,1:T(8,128)}, u32[]{:S(2)}) copy-start(f32[256,512]{0,1:T(8,128)} %copy-done.7) | copy-start | bytes 1572868
  471.4 22.3 %copy-start.6 = (f32[256,512]{0,1:T(8,128)S(1)}, f32[256,512]{0,1:T(8,128)}, u32[]{:S(2)}) copy-start(f32[256,512]{0,1:T(8,128)} %copy-done.5) | copy-start | bytes 1572868
  471.4 22.8 %copy-start.2 = (f32[256,512]{0,1:T(8,128)S(1)}, f32[256,512]{0,1:T(8,128)}, u32[]{:S(2)}) copy-start(f32[256,512]{0,1:T(8,128)} %copy-done.1) | copy-start | bytes 1572868
  471.4 22.9 %copy-start.4 = (f32[256,512]{0,1:T(8,128)S(1)}, f32[256,512]{0,1:T(8,128)}, u32[]{:S(2)}) copy-start(f32[256,512]{0,1:T(8,128)} %copy-done.3) | copy-start | bytes 1572868
  471.5 19.9 %collective-permute-start.14 = (f32[256,512]{0,1:T(8,128)}, f32[256,512]{0,1:T(8,128)S(1)}, u32[]{:S(2)}, u32[]{:S(2)}) collective-permute-start(f32[256,512]{0,1:T(8,128)} %collective-permute-done.13), channel_id=1, source_target_pairs={{0,120},{8,0},{16,8},{24,16},{32,24},{40,32},{48,40},{56,48},{64,5... | collective-permute-start | bytes 1572872 | tf_op jit(solution)/shard_map/ppermute | solution.py:15
Sparse Core Ops, SparseCore 0:
  10.1 45.0 all-gather.6
  57.4 42.2 all-gather.10
  101.8 42.4 all-gather.8
  363.0 31.3 all-gather.14
  395.9 31.9 all-gather.12
  429.9 93.8 all-gather.16
